TPU v7x, 32 devices: a whole 2x2x4 slice. The times are simulated.
32 devices in a mesh: grp: 1, ex: 32 (over z, y, x, core).
Axes of the slice: x: 2, y: 2, z: 4, core: 2. Of those that a mesh axis runs over, the one named last changes fastest.
Arguments:
- example_inputs: bfloat16 [32, 1024, 4096], P(('grp', 'ex')), may hold values from -70 to 70, as said below
- output_grads: bfloat16 [32, 1024, 1024], P(('grp', 'ex')), may hold values from -70 to 70, as said below
- proj_in: bfloat16 [128, 4096], replicated, may hold values from -0.09375 to 0.09375
- proj_out: bfloat16 [64, 1024], replicated, may hold values from -0.1875 to 0.1875
- test_grads: bfloat16 [128, 8192], P('ex'), may hold values from -6 to 6
Outputs:
- scores: float32 [32, 128], P(('grp', 'ex'))
Inputs may be any that keep to these rules, and one draw needn't show every extreme that they name: `example_inputs`: entries of the candidates' layer inputs lie within this range. `output_grads`: entries of the output gradients lie within this range.
All inputs are finite; a program needn't handle non-finite values.
Results may differ from a plain program's by a relative error of at most 0.0082.
Values may be sent and summed in bfloat16 or wider, within the bound.
A program may use at most 128 MiB of HBM per device.

v0:
```python
import jax
import jax.numpy as jnp
from jax import lax
from jax.sharding import PartitionSpec as P

K_IN = 128
K_OUT = 64
TOK_EX = 1024


def damped_inverse(cov, width):
    identity = jnp.eye(width, dtype=jnp.float32)
    damped = cov + 0.1 * jnp.trace(cov) / width * identity
    factor = jnp.linalg.cholesky(damped)
    lower_inv = lax.linalg.triangular_solve(factor, identity, left_side=True, lower=True)
    return jnp.dot(lower_inv.T, lower_inv, precision=lax.Precision.HIGHEST)


def on_device(example_inputs, output_grads, proj_in, proj_out, test_grads):
    examples_here = example_inputs.shape[0]
    devices = lax.axis_size("ex")
    feat_proj = jnp.einsum(
        "etd,kd->etk", example_inputs, proj_in, preferred_element_type=jnp.float32
    ).astype(jnp.bfloat16)
    grad_proj = jnp.einsum(
        "etv,kv->etk", output_grads, proj_out, preferred_element_type=jnp.float32
    ).astype(jnp.bfloat16)
    grads = jnp.einsum("eto,eti->eoi", grad_proj, feat_proj, preferred_element_type=jnp.float32)
    flat_feat = feat_proj.reshape(-1, K_IN)
    flat_grad = grad_proj.reshape(-1, K_OUT)
    local_in = jnp.einsum("ti,tj->ij", flat_feat, flat_feat, preferred_element_type=jnp.float32)
    local_out = jnp.einsum("ti,tj->ij", flat_grad, flat_grad, preferred_element_type=jnp.float32)
    sum_in, sum_out = lax.psum((local_in, local_out), "ex")
    total_tokens = examples_here * TOK_EX * devices
    inverse_in = damped_inverse(sum_in / total_tokens, K_IN)
    inverse_out = damped_inverse(sum_out / total_tokens, K_OUT)
    scale = 4.0 / (K_IN * K_OUT * TOK_EX) ** 0.5
    left = jnp.einsum("oa,eai->eoi", inverse_out, grads, precision=lax.Precision.HIGHEST)
    both = jnp.einsum("eoa,ai->eoi", left, inverse_in, precision=lax.Precision.HIGHEST)
    precond = both.reshape(grads.shape[0], K_OUT * K_IN).astype(jnp.bfloat16)
    score_block = lax.dot_general(
        precond,
        lax.all_gather(test_grads, "ex", axis=0, tiled=True),
        (((1,), (1,)), ((), ())),
        preferred_element_type=jnp.float32,
    )
    return score_block * scale


def solution(mesh):
    return jax.shard_map(
        on_device,
        mesh=mesh,
        in_specs=(
            P(("grp", "ex"), None, None),
            P(("grp", "ex"), None, None),
            P(),
            P(),
            P("ex", None),
        ),
        out_specs=P(("grp", "ex"), None),
        check_vma=False,
    )
```

profile of v0, /device:TPU:0, one launch (start us, length us, event | category | flops | bytes accessed | tf_op | source)
XLA Modules:
  0.0 210.4 jit_solution(5839962891657765232)
XLA Ops:
  6.5 0.0 copy-start
  6.5 0.0 copy-start.1
  6.5 0.0 all-reduce.2.cloned.1.call-start
  6.5 6.1 %fusion.4 = bf16[1024,128]{1,0:T(8,128)(2,1)S(1)} fusion(bf16[128,4096]{1,0:T(8,128)(2,1)} %param.7, bf16[1,1024,4096]{2,1,0:T(8,128)(2,1)} %param.5), kind=kOutput, calls=%fused_computation.4 | convolution fusion | flops 1073872896 | bytes 9699328 | tf_op jit(solution)/shard_map/etd,kd->etk/dot_general | solution.py:22
  12.6 0.9 fusion.24
  13.5 0.0 all-reduce.2.cloned.1.call-update
  13.6 0.0 all-gather.3.cloned.1.call-start
  13.6 0.7 all-gather.3.cloned.1.call-update
  14.3 0.0 copy-done
  14.3 0.0 copy-done.1
  14.3 0.8 fusion.7
  15.1 0.2 fusion.22
  15.3 42.3 %psum.14 = f32[64,64]{1,0:T(8,128)S(1)} all-reduce(f32[64,64]{1,0:T(8,128)S(1)} %fusion.22), channel_id=1, replica_groups=mesh['grp'=1,'ex'=32] {'ex'}, use_global_device_ids=true, to_apply=%region_0.0 | all-reduce | flops 4096 | bytes 32768 | tf_op jit(solution)/shard_map/psum | solution.py:33
  57.6 0.6 select_reduce_fusion.3
  58.9 0.1 copy.8
  59.0 5.8 %cholesky.33 = f32[64,64]{1,0:T(8,128)S(1)} custom-call(f32[64,64]{1,0:T(8,128)S(1)} %fusion.20), custom_call_target="Cholesky" | custom-call | tf_op jit(solution)/shard_map/jit(cholesky)/cholesky | solution.py:14
  64.9 0.6 compare_reduce_fusion.1
  65.5 0.7 fusion.17
  66.2 4.9 %custom-call.12 = f32[1,64,64]{1,2,0:T(8,128)S(1)} custom-call(f32[1,64,64]{2,1,0:T(8,128)S(1)} %fusion.17), custom_call_target="InvertDiagBlocksLowerTriangular" | custom-call | tf_op jit(solution)/shard_map/triangular_solve | solution.py:15
  71.1 0.2 fusion.18
  71.3 0.2 fusion.23
  71.5 0.2 fusion.21
  71.7 0.2 convolution_bitcast_fusion
  71.9 64.2 %all-reduce.2.cloned.1.call-done = f32[128,128]{1,0:T(8,128)} async-done(((f32[128,128]{1,0:T(8,128)}), f32[128,128]{1,0:T(8,128)}) %all-reduce.2.cloned.1.call-update) | async-done | bytes 65552 | tf_op jit(solution)/shard_map/psum | solution.py:33
  136.0 1.5 select_reduce_fusion.1
  138.2 0.9 select_add_fusion
  139.0 0.1 copy.9
  139.1 0.9 fusion.16
  140.0 11.7 %cholesky.68 = f32[128,128]{1,0:T(8,128)S(1)} custom-call(f32[128,128]{1,0:T(8,128)S(1)} %fusion.16), custom_call_target="Cholesky" | custom-call | tf_op jit(solution)/shard_map/jit(cholesky)/cholesky | solution.py:14
  151.7 0.6 compare_reduce_fusion
  152.4 0.7 fusion.13
  153.0 9.8 %custom-call.13 = f32[1,128,128]{1,2,0:T(8,128)S(1)} custom-call(f32[1,128,128]{2,1,0:T(8,128)S(1)} %fusion.13), custom_call_target="InvertDiagBlocksLowerTriangular" | custom-call | tf_op jit(solution)/shard_map/triangular_solve | solution.py:15
  162.9 0.3 fusion.14
  163.1 0.3 fusion.25
  163.4 0.2 fusion.10
  163.6 33.2 %all-gather.3.cloned.1.call-done = bf16[32,4,8192]{2,1,0:T(4,128)(2,1)} async-done(((bf16[1,4,8192]{2,1,0:T(4,128)(2,1)}), bf16[32,4,8192]{2,1,0:T(4,128)(2,1)}) %all-gather.3.cloned.1.call-update) | async-done | bytes 2097168 | tf_op jit(solution)/shard_map/all_gather | solution.py:43
  196.8 4.0 %reshape.57 = bf16[128,8192]{1,0:T(8,128)(2,1)} reshape(bf16[32,4,8192]{2,1,0:T(4,128)(2,1)} %all-gather.3.cloned.1.call-done) | data formatting | bytes 4194304
  200.8 2.8 %fusion.12 = f32[1,128]{1,0:T(1,128)} fusion(bf16[8192,1]{0,1:T(2,128)(2,1)S(1)} %reshape.58, bf16[128,8192]{1,0:T(8,128)(2,1)} %reshape.57), kind=kOutput, calls=%fused_computation.11 | convolution fusion | flops 2097280 | bytes 2114048 | tf_op jit(solution)/shard_map/dot_general | solution.py:41
  (5 shorter events, 0.1 us)
Async XLA Ops:
  6.5 7.8 %copy-start = (bf16[1,1024,1024]{2,1,0:T(8,128)(2,1)S(1)}, bf16[1,1024,1024]{2,1,0:T(8,128)(2,1)}, u32[]{:S(2)}) copy-start(bf16[1,1024,1024]{2,1,0:T(8,128)(2,1)} %param.6) | copy-start | bytes 6291460
  6.5 7.8 %copy-start.1 = (bf16[64,1024]{1,0:T(8,128)(2,1)S(1)}, bf16[64,1024]{1,0:T(8,128)(2,1)}, u32[]{:S(2)}) copy-start(bf16[64,1024]{1,0:T(8,128)(2,1)} %param.8) | copy-start | bytes 393220
  6.5 129.5 %all-reduce.2.cloned.1.call-start = ((), (), s32[]{:S(2)}) async-start(), calls=%async_computation | async-start | bytes 131072 | tf_op jit(solution)/shard_map/psum | solution.py:33
  13.6 183.3 %all-gather.3.cloned.1.call-start = ((), (), s32[]{:S(2)}) async-start(), calls=%async_computation.1 | async-start | bytes 2162688 | tf_op jit(solution)/shard_map/all_gather | solution.py:43
Sparse Core Ops, SparseCore 0:
  13.7 122.3 all-reduce.1
  138.9 57.8 all-gather.2
where the time goes:
time: 211 us; the launch traced here: 210 us
  waiting for transfers between devices  98.1 us (46%)
  blocking collectives  42.3 us (20%)
  other arithmetic  38.8 us (18%)
  between operations  14.9 us (7%)
  matrix products  12.2 us (6%)
  local copies, waits for them, and re-layouts  4.16 us (2%)
    psum x1, waiting for transfers between devices, on_device(): sum_in, sum_out = lax.psum((local_in, local_out), 'ex')  64.2 us
    psum x1, blocking collectives, on_device(): sum_in, sum_out = lax.psum((local_in, local_out), 'ex')  42.3 us
    all_gather x1, waiting for transfers between devices, on_device(): lax.all_gather(test_grads, 'ex', axis=0, tiled=True)  33.2 us
    another operation x6, other arithmetic, damped_inverse(): factor = jnp.linalg.cholesky(damped)  18.9 us
    another operation x4, other arithmetic, damped_inverse(): lax.linalg.triangular_solve(factor, identity, left_side=True, lower=True)  16 us
    dot_general x1, matrix products, on_device(): jnp.einsum('etd,kd->etk', example_inputs, proj_in, preferred_element_type...  6.09 us
  transfers between devices with their start and end apart: 2, of which 2 were waited for; matrix products, arithmetic and copies ran while one was open for 20% of the time, Pallas kernels for 0%

commit v1 on v0

v1 whole, which is shorter than its diff:
```python
import functools
import math

import jax
import jax.numpy as jnp
from jax import lax
from jax.experimental import pallas as pl
from jax.experimental.pallas import tpu as pltpu
from jax.sharding import PartitionSpec as P

MESH = pl.DeviceIdType.MESH
HIGHEST = lax.Precision.HIGHEST
F32 = jnp.float32
BF16 = jnp.bfloat16
DAMP = 0.1
NT = (((1,), (1,)), ((), ()))
TN = (((0,), (0,)), ((), ()))


def eye(n):
    return lax.broadcasted_iota(jnp.int32, (n, n), 0) == lax.broadcasted_iota(
        jnp.int32, (n, n), 1
    )


def split(a):
    hi = a.astype(BF16)
    lo = (a - hi.astype(F32)).astype(BF16)
    return hi, lo


def wide_dot(a, b):
    n = b.shape[1]
    row = jnp.concatenate(split(b), axis=1)
    both = jnp.dot(
        jnp.concatenate(split(a), axis=1),
        jnp.concatenate([row, row], axis=0),
        preferred_element_type=F32,
    )
    return both[:, :n] + both[:, n:]


def plan(n, target=1e-3):
    low, high = DAMP / n, 1.0 + DAMP / n
    err = (high - low) / (high + low)
    factors = []
    while err > target:
        factors.append(2.0 / (2.0 - err * err))
        err = err * err / (2.0 - err * err)
    return 2.0 / (high + low), factors


def inverses(sums):
    state = []
    for s in sums:
        n = s.shape[0]
        diag = eye(n)
        trace = jnp.sum(
            jnp.sum(jnp.where(diag, s, 0.0), axis=1, keepdims=True), axis=0, keepdims=True
        )
        inv_trace = 1.0 / trace
        b = s * inv_trace + jnp.where(diag, DAMP / n, 0.0)
        first, factors = plan(n)
        x = jnp.where(diag, first, 0.0)
        y = first * b
        state.append([b, x, y, inv_trace, factors])
    for step in range(max(len(st[4]) for st in state)):
        for st in state:
            b, x, y, _, factors = st
            if step >= len(factors):
                continue
            n = b.shape[0]
            c = factors[step]
            if step == 0:
                yy = wide_dot(y, y)
                xy = x[0:1, 0:1] * y
            else:
                prod = wide_dot(jnp.concatenate([x, y], axis=0), y)
                xy, yy = prod[:n], prod[n:]
            st[1] = c * (2.0 * x - xy)
            st[2] = c * (2.0 * y - yy)
    out = []
    for b, x, _, inv_trace, _ in state:
        n = b.shape[0]
        rest = jnp.where(eye(n), 1.0, 0.0) - jnp.dot(
            b, x, precision=HIGHEST, preferred_element_type=F32
        )
        out.append((x + wide_dot(x, rest)) * inv_trace)
    return out


def kernel(
    inner, outer, chunks, tokens, scale,
    x_hbm, g_hbm, pin_hbm, pout_hbm, test_hbm, out_ref,
    x_buf, g_buf, pin_buf, pout_buf, tests, cov, moments, rs_buf, z_buf, full, grads,
    pre, flat, sbuf, rbuf,
    in_sem, t_send, t_recv, rs_send, rs_recv, g_send, g_recv, z_send, z_recv,
    ag_send, ag_recv, s_send, s_recv,
):
    k_in, k_out = pin_buf.shape[0], pout_buf.shape[0]
    me = lax.axis_index("ex")
    p, z = lax.rem(me, inner), lax.div(me, inner)
    rows = moments.shape[0] // inner
    step_rows = x_buf.shape[1]

    def at_inner(k):
        return z * inner + lax.rem(p + k, inner)

    def at_outer(k):
        return lax.rem(z + k, outer) * inner + p

    def remote(src, dst, send, recv, device):
        return pltpu.make_async_remote_copy(
            src_ref=src, dst_ref=dst, send_sem=send, recv_sem=recv,
            device_id={"ex": device}, device_id_type=MESH,
        )

    barrier = pltpu.get_barrier_semaphore()
    for k in range(1, inner):
        pl.semaphore_signal(barrier, inc=1, device_id={"ex": at_inner(k)}, device_id_type=MESH)
    for k in range(1, outer):
        pl.semaphore_signal(barrier, inc=1, device_id={"ex": at_outer(k)}, device_id_type=MESH)

    loads = [
        pltpu.make_async_copy(pout_hbm, pout_buf, in_sem.at[0]),
        pltpu.make_async_copy(g_hbm, g_buf, in_sem.at[1]),
        pltpu.make_async_copy(pin_hbm, pin_buf, in_sem.at[2]),
    ]
    own_tests = pltpu.make_async_copy(test_hbm, tests.at[z], in_sem.at[3])

    def x_load(i):
        return pltpu.make_async_copy(
            x_hbm.at[pl.ds(i * step_rows, step_rows)], x_buf.at[i], in_sem.at[4 + i]
        )

    for c in loads:
        c.start()
    own_tests.start()
    for i in range(chunks):
        x_load(i).start()

    pl.semaphore_wait(barrier, inner + outer - 2)
    test_copies = [
        remote(test_hbm, tests.at[z], t_send.at[k], t_recv.at[k], at_outer(k))
        for k in range(1, outer)
    ]
    for c in test_copies:
        c.start()

    for c in loads:
        c.wait()
    cov[...] = jnp.zeros_like(cov)

    def project(i, carry):
        begin = pl.multiple_of(i * step_rows, step_rows)
        back = lax.dot_general(
            g_buf[pl.ds(begin, step_rows), :], pout_buf[...], NT, preferred_element_type=F32
        ).astype(BF16)
        x_load(i).wait()
        feat = lax.dot_general(
            x_buf[i], pin_buf[...], NT, preferred_element_type=F32
        ).astype(BF16)
        both = jnp.concatenate([feat, back], axis=1)
        cov[...] += lax.dot_general(both, both, TN, preferred_element_type=F32)
        return carry

    lax.fori_loop(0, chunks, project, 0)

    moments[0:k_in, :] = cov[0:k_in, 0:k_in]
    moments[k_in : k_in + k_out, :] = jnp.concatenate(
        [cov[k_in : k_in + k_out, k_in : k_in + k_out], jnp.zeros((k_out, k_in - k_out), F32)],
        axis=1,
    )
    grads[p] = cov[k_in : k_in + k_out, 0:k_in]

    rs_copies = []
    for k in range(1, inner):
        peer = lax.rem(p + k, inner)
        rs_copies.append(
            remote(
                moments.at[pl.ds(pl.multiple_of(peer * rows, 8), rows)],
                rs_buf.at[p], rs_send.at[k], rs_recv.at[k], at_inner(k),
            )
        )
    for c in rs_copies:
        c.start()
    rs_buf[p] = moments[pl.ds(pl.multiple_of(p * rows, 8), rows), :]
    for c in rs_copies:
        c.wait_recv()
    part = rs_buf[0]
    for j in range(1, inner):
        part = part + rs_buf[j]
    z_buf[z] = part
    z_copies = [
        remote(z_buf.at[z], z_buf.at[z], z_send.at[k], z_recv.at[k], at_outer(k))
        for k in range(1, outer)
    ]
    for c in z_copies:
        c.start()
    g_copies = [
        remote(grads.at[p], grads.at[p], g_send.at[k], g_recv.at[k], at_inner(k))
        for k in range(1, inner)
    ]
    for c in g_copies:
        c.start()
    for c in z_copies:
        c.wait_recv()
    total = z_buf[0]
    for j in range(1, outer):
        total = total + z_buf[j]
    mine = full.at[pl.ds(pl.multiple_of(p * rows, 8), rows)]
    mine[...] = total
    ag_copies = [
        remote(mine, mine, ag_send.at[k], ag_recv.at[k], at_inner(k)) for k in range(1, inner)
    ]
    for c in ag_copies:
        c.start()
    for c in g_copies:
        c.wait_recv()
    for c in ag_copies:
        c.wait_recv()

    sum_in = full[0:k_in, :]
    sum_out = full[k_in : k_in + k_out, 0:k_out]
    inv_in, inv_out = inverses([sum_in, sum_out])
    inv_in = inv_in * tokens
    inv_out = inv_out * tokens
    right = jnp.dot(
        grads[...].reshape(inner * k_out, k_in), inv_in,
        precision=HIGHEST, preferred_element_type=F32,
    )
    for e in range(inner):
        pre[e * k_out : (e + 1) * k_out, :] = jnp.dot(
            inv_out, right[e * k_out : (e + 1) * k_out],
            precision=HIGHEST, preferred_element_type=F32,
        )
    for o in range(k_out):
        flat[:, o * k_in : (o + 1) * k_in] = pre[pl.ds(o, inner, stride=k_out), :]
    precond = flat[...].astype(BF16)

    own_tests.wait()
    for c in test_copies:
        c.wait_recv()
    per = tests.shape[1]
    width = out_ref.shape[1]
    placed = jnp.zeros((inner, width), F32)
    for j in range(outer):
        block = lax.dot_general(precond, tests[j], NT, preferred_element_type=F32)
        first = (j * inner + p) * per
        put = lax.broadcasted_iota(jnp.int32, (per, width), 1) == (
            first + lax.broadcasted_iota(jnp.int32, (per, width), 0)
        )
        placed = placed + jnp.dot(
            block, jnp.where(put, 1.0, 0.0), precision=HIGHEST, preferred_element_type=F32
        )
    for e in range(inner):
        sbuf[e] = placed[e : e + 1]
    s_copies = [
        remote(
            sbuf.at[lax.rem(p + k, inner)], rbuf.at[p], s_send.at[k], s_recv.at[k], at_inner(k)
        )
        for k in range(1, inner)
    ]
    for c in s_copies:
        c.start()
    rbuf[p] = sbuf[p]
    for c in s_copies:
        c.wait_recv()
    score = rbuf[0]
    for j in range(1, inner):
        score = score + rbuf[j]
    out_ref[...] = score * scale
    for group in (test_copies, rs_copies, z_copies, g_copies, ag_copies, s_copies):
        for c in group:
            c.wait_send()


def on_device(devices, x, g, proj_in, proj_out, tests):
    _, tok, _ = x.shape
    k_in, k_out = proj_in.shape[0], proj_out.shape[0]
    inner = math.gcd(devices, 8)
    outer = devices // inner
    per = tests.shape[0]
    chunks = 4
    total_tokens = tok * devices
    scale = 4.0 / (k_in * k_out * tok) ** 0.5
    height = k_in + k_out
    any_space = pl.BlockSpec(memory_space=pl.ANY)
    dma = pltpu.SemaphoreType.DMA
    return pl.pallas_call(
        functools.partial(kernel, inner, outer, chunks, float(total_tokens), scale),
        out_shape=jax.ShapeDtypeStruct((1, per * devices), F32),
        in_specs=[any_space] * 5,
        out_specs=pl.BlockSpec(memory_space=pltpu.VMEM),
        scratch_shapes=[
            pltpu.VMEM((chunks, tok // chunks, x.shape[2]), BF16),
            pltpu.VMEM(g.shape[1:], BF16),
            pltpu.VMEM(proj_in.shape, BF16),
            pltpu.VMEM(proj_out.shape, BF16),
            pltpu.VMEM((outer,) + tests.shape, BF16),
            pltpu.VMEM((height, height), F32),
            pltpu.VMEM((height, k_in), F32),
            pltpu.VMEM((inner, height // inner, k_in), F32),
            pltpu.VMEM((outer, height // inner, k_in), F32),
            pltpu.VMEM((height, k_in), F32),
            pltpu.VMEM((inner, k_out, k_in), F32),
            pltpu.VMEM((inner * k_out, k_in), F32),
            pltpu.VMEM((inner, k_out * k_in), F32),
            pltpu.VMEM((inner, 1, per * devices), F32),
            pltpu.VMEM((inner, 1, per * devices), F32),
            dma((4 + chunks,)),
            dma((outer,)), dma((outer,)),
            dma((inner,)), dma((inner,)),
            dma((inner,)), dma((inner,)),
            dma((outer,)), dma((outer,)),
            dma((inner,)), dma((inner,)),
            dma((inner,)), dma((inner,)),
        ],
        compiler_params=pltpu.CompilerParams(
            collective_id=0, has_side_effects=True, vmem_limit_bytes=56 * 1024 * 1024
        ),
    )(x[0], g[0], proj_in, proj_out, tests)


def solution(mesh):
    return jax.shard_map(
        functools.partial(on_device, mesh.shape["ex"]),
        mesh=mesh,
        in_specs=(
            P(("grp", "ex"), None, None),
            P(("grp", "ex"), None, None),
            P(),
            P(),
            P("ex", None),
        ),
        out_specs=P(("grp", "ex"), None),
        check_vma=False,
    )
```

time: 211 us -> 33 us (0.16)
  waiting for transfers between devices: 98.1 us -> 0 us
  blocking collectives: 42.3 us -> 0 us
  other arithmetic: 38.8 us -> 0 us
  Pallas kernels: 0 us -> 31.7 us
  between operations: 14.9 us -> 0.01 us
  matrix products: 12.2 us -> 0 us
  local copies, waits for them, and re-layouts: 4.16 us -> 1.19 us
    psum x1 -> x0, waiting for transfers between devices: 64.2 us -> none  [on_device(): sum_in, sum_out = lax.psum((local_in, local_out), 'ex')]
    psum x1 -> x0, blocking collectives: 42.3 us -> none  [on_device(): sum_in, sum_out = lax.psum((local_in, local_out), 'ex')]
    another operation x10 -> x0, other arithmetic: 34.9 us -> none  [the longest x6 18.9 us: damped_inverse(): factor = jnp.linalg.cholesky(damped)]
    all_gather x1 -> x0, waiting for transfers between devices: 33.2 us -> none  [on_device(): lax.all_gather(test_grads, 'ex', axis=0, tiled=True)]
    pallas_call x0 -> x1, Pallas kernels: none -> 31.7 us  [on_device(): pl.pallas_call(functools.partial(kernel, inner, outer, chunks, float(tota...]
    dot_general x10 -> x0, matrix products: 11.7 us -> none  [the longest x1 6.09 us: on_device(): jnp.einsum('etd,kd->etk', example_inputs, proj_in, preferred_element_type...]
    unnamed x5 -> x1, local copies, waits for them, and re-layouts: 3.98 us -> 1.19 us
  transfers between devices with their start and end apart: 2 -> 0, of which waited for: 2 -> 0; matrix products, arithmetic and copies ran while one was open for 20% -> 0% of each run, Pallas kernels for 0% -> 0%
where the time goes in v1:
time: 33 us; the launch traced here: 32.9 us
  Pallas kernels  31.7 us (96%)
  local copies, waits for them, and re-layouts  1.19 us (4%)
    pallas_call x1, Pallas kernels, on_device(): pl.pallas_call(functools.partial(kernel, inner, outer, chunks, float(tota...  31.7 us
    unnamed x1, local copies, waits for them, and re-layouts  1.19 us

profile of v1, /device:TPU:0, one launch (start us, length us, event | category | flops | bytes accessed | tf_op | source)
XLA Modules:
  0.0 32.9 jit_solution(5093975289999983621)
XLA Ops:
  0.0 31.7 %shard_map.55 = f32[1,128]{1,0:T(1,128)} custom-call(bf16[1024,4096]{1,0:T(8,128)(2,1)} %bitcast.2, bf16[1024,1024]{1,0:T(8,128)(2,1)} %bitcast.3, bf16[128,4096]{1,0:T(8,128)(2,1)} %pin_hbm.1, bf16[64,1024]{1,0:T(8,128)(2,1)} %pout_hbm.1, bf16[4,8192]{1,0:T(4,128)(2,1)} %test_hbm.1), custom_call_target="tpu_custom_call" | custom-call | tf_op jit(solution)/shard_map/pallas_call | solution.py:290
  31.7 1.2 %copy.7 = f32[1,128]{1,0:T(1,128)} copy(f32[1,128]{1,0:T(1,128)} %shard_map.55) | data formatting | bytes 1024

commit v2 on v1

--- a/solution.py
+++ b/solution.py
@@ -40,7 +40,7 @@
     return both[:, :n] + both[:, n:]
 
 
-def plan(n, target=1e-3):
+def plan(n, target=2e-3):
     low, high = DAMP / n, 1.0 + DAMP / n
     err = (high - low) / (high + low)
     factors = []
@@ -52,35 +52,38 @@
 
 def inverses(sums):
     state = []
-    for s in sums:
-        n = s.shape[0]
-        diag = eye(n)
+    for s, n in sums:
+        size = s.shape[0]
+        diag = eye(size)
         trace = jnp.sum(
             jnp.sum(jnp.where(diag, s, 0.0), axis=1, keepdims=True), axis=0, keepdims=True
         )
         inv_trace = 1.0 / trace
         b = s * inv_trace + jnp.where(diag, DAMP / n, 0.0)
         first, factors = plan(n)
+        if size > n:
+            beyond = lax.broadcasted_iota(jnp.int32, (size, size), 0) >= n
+            b = jnp.where(diag & beyond, 1.0 / first, b)
         x = jnp.where(diag, first, 0.0)
         y = first * b
-        state.append([b, x, y, inv_trace, factors])
+        state.append([b, x, y, inv_trace, factors, first])
     for step in range(max(len(st[4]) for st in state)):
         for st in state:
-            b, x, y, _, factors = st
+            b, x, y, _, factors, plan_first = st
             if step >= len(factors):
                 continue
             n = b.shape[0]
             c = factors[step]
             if step == 0:
                 yy = wide_dot(y, y)
-                xy = x[0:1, 0:1] * y
+                xy = plan_first * y
             else:
                 prod = wide_dot(jnp.concatenate([x, y], axis=0), y)
                 xy, yy = prod[:n], prod[n:]
             st[1] = c * (2.0 * x - xy)
             st[2] = c * (2.0 * y - yy)
     out = []
-    for b, x, _, inv_trace, _ in state:
+    for b, x, _, inv_trace, _, _ in state:
         n = b.shape[0]
         rest = jnp.where(eye(n), 1.0, 0.0) - jnp.dot(
             b, x, precision=HIGHEST, preferred_element_type=F32
@@ -90,10 +93,10 @@
 
 
 def kernel(
-    inner, outer, chunks, tokens, scale,
+    inner, outer, chunks, tokens,
     x_hbm, g_hbm, pin_hbm, pout_hbm, test_hbm, out_ref,
     x_buf, g_buf, pin_buf, pout_buf, tests, cov, moments, rs_buf, z_buf, full, grads,
-    pre, flat, sbuf, rbuf,
+    pre, flat, sbuf, rbuf, acc,
     in_sem, t_send, t_recv, rs_send, rs_recv, g_send, g_recv, z_send, z_recv,
     ag_send, ag_recv, s_send, s_recv,
 ):
@@ -101,7 +104,7 @@
     me = lax.axis_index("ex")
     p, z = lax.rem(me, inner), lax.div(me, inner)
     rows = moments.shape[0] // inner
-    step_rows = x_buf.shape[1]
+    step_cols = x_buf.shape[2]
 
     def at_inner(k):
         return z * inner + lax.rem(p + k, inner)
@@ -123,54 +126,74 @@
 
     loads = [
         pltpu.make_async_copy(pout_hbm, pout_buf, in_sem.at[0]),
-        pltpu.make_async_copy(g_hbm, g_buf, in_sem.at[1]),
-        pltpu.make_async_copy(pin_hbm, pin_buf, in_sem.at[2]),
-    ]
-    own_tests = pltpu.make_async_copy(test_hbm, tests.at[z], in_sem.at[3])
+        pltpu.make_async_copy(pin_hbm, pin_buf, in_sem.at[1]),
+    ]
+    own_tests = pltpu.make_async_copy(test_hbm, tests.at[z], in_sem.at[2])
 
     def x_load(i):
         return pltpu.make_async_copy(
-            x_hbm.at[pl.ds(i * step_rows, step_rows)], x_buf.at[i], in_sem.at[4 + i]
-        )
-
-    for c in loads:
-        c.start()
+            x_hbm.at[:, i * step_cols : (i + 1) * step_cols], x_buf.at[i], in_sem.at[5 + i]
+        )
+
+    mid = g_buf.shape[0] // 2
+    quarter = mid // 2
+    g_loads = [
+        pltpu.make_async_copy(
+            g_hbm.at[pl.ds(h * mid, mid)], g_buf.at[pl.ds(h * mid, mid)], in_sem.at[3 + h]
+        )
+        for h in range(2)
+    ]
+    loads[0].start()
+    for c in g_loads:
+        c.start()
+    loads[1].start()
     own_tests.start()
     for i in range(chunks):
         x_load(i).start()
 
-    pl.semaphore_wait(barrier, inner + outer - 2)
     test_copies = [
         remote(test_hbm, tests.at[z], t_send.at[k], t_recv.at[k], at_outer(k))
         for k in range(1, outer)
     ]
-    for c in test_copies:
-        c.start()
-
-    for c in loads:
-        c.wait()
-    cov[...] = jnp.zeros_like(cov)
-
-    def project(i, carry):
-        begin = pl.multiple_of(i * step_rows, step_rows)
-        back = lax.dot_general(
-            g_buf[pl.ds(begin, step_rows), :], pout_buf[...], NT, preferred_element_type=F32
-        ).astype(BF16)
+    loads[0].wait()
+    halves = (slice(0, mid), slice(mid, 2 * mid))
+    backs = []
+    for h in range(2):
+        g_loads[h].wait()
+        backs += [
+            lax.dot_general(
+                g_buf[q : q + quarter, :], pout_buf[...], NT, preferred_element_type=F32
+            ).astype(BF16)
+            for q in (h * mid, h * mid + quarter)
+        ]
+    loads[1].wait()
+    for i in range(chunks):
         x_load(i).wait()
-        feat = lax.dot_general(
-            x_buf[i], pin_buf[...], NT, preferred_element_type=F32
-        ).astype(BF16)
-        both = jnp.concatenate([feat, back], axis=1)
-        cov[...] += lax.dot_general(both, both, TN, preferred_element_type=F32)
-        return carry
-
-    lax.fori_loop(0, chunks, project, 0)
-
-    moments[0:k_in, :] = cov[0:k_in, 0:k_in]
-    moments[k_in : k_in + k_out, :] = jnp.concatenate(
-        [cov[k_in : k_in + k_out, k_in : k_in + k_out], jnp.zeros((k_out, k_in - k_out), F32)],
-        axis=1,
-    )
+        if i == 1:
+            pl.semaphore_wait(barrier, inner + outer - 2)
+            for c in test_copies:
+                c.start()
+        weights = pin_buf[:, i * step_cols : (i + 1) * step_cols]
+        feats = [
+            lax.dot_general(x_buf[i, h, :], weights, NT, preferred_element_type=F32)
+            for h in halves
+        ]
+        for h, feat in zip(halves, feats):
+            if i == 0:
+                acc[h, :] = feat
+            else:
+                acc[h, :] += feat
+    parts = []
+    for h in range(2):
+        back = jnp.concatenate(backs[2 * h : 2 * h + 2], axis=0)
+        both = jnp.concatenate([acc[halves[h], :].astype(BF16), back], axis=1)
+        parts.append(lax.dot_general(both, both, TN, preferred_element_type=F32))
+    cov[...] = parts[0] + parts[1]
+
+    half = k_in // 2
+    moments[0:half, :] = cov[0:half, 0:k_in]
+    moments[half:k_in, half:k_in] = cov[half:k_in, half:k_in]
+    moments[half:k_in, 0:half] = cov[k_in : k_in + k_out, k_in : k_in + k_out]
     grads[p] = cov[k_in : k_in + k_out, 0:k_in]
 
     rs_copies = []
@@ -201,8 +224,6 @@
         remote(grads.at[p], grads.at[p], g_send.at[k], g_recv.at[k], at_inner(k))
         for k in range(1, inner)
     ]
-    for c in g_copies:
-        c.start()
     for c in z_copies:
         c.wait_recv()
     total = z_buf[0]
@@ -216,24 +237,35 @@
     for c in ag_copies:
         c.start()
     for c in g_copies:
-        c.wait_recv()
+        c.start()
     for c in ag_copies:
         c.wait_recv()
 
-    sum_in = full[0:k_in, :]
-    sum_out = full[k_in : k_in + k_out, 0:k_out]
-    inv_in, inv_out = inverses([sum_in, sum_out])
+    top, low = full[0:half, :], full[half:k_in, :]
+    corner = jnp.concatenate([top.T[half:k_in, :], low[:, half:]], axis=1)
+    sum_in = jnp.concatenate([top, corner], axis=0)
+    sum_out = jnp.concatenate([low[:, 0:half], jnp.zeros((half, half), F32)], axis=1)
+    sum_out = jnp.concatenate([sum_out, jnp.zeros((half, k_in), F32)], axis=0)
+    inv_in, inv_out = inverses([(sum_in, k_in), (sum_out, k_out)])
     inv_in = inv_in * tokens
-    inv_out = inv_out * tokens
-    right = jnp.dot(
-        grads[...].reshape(inner * k_out, k_in), inv_in,
-        precision=HIGHEST, preferred_element_type=F32,
-    )
-    for e in range(inner):
-        pre[e * k_out : (e + 1) * k_out, :] = jnp.dot(
-            inv_out, right[e * k_out : (e + 1) * k_out],
+    inv_out = inv_out[0:k_out, 0:k_out] * tokens
+    for c in g_copies:
+        c.wait_recv()
+    batch = max(inner // 2, 1)
+    rights = [
+        jnp.dot(
+            grads[e : e + batch].reshape(batch * k_out, k_in), inv_in,
             precision=HIGHEST, preferred_element_type=F32,
         )
+        for e in range(0, inner, batch)
+    ]
+    for e in range(batch):
+        for r, right in enumerate(rights):
+            at = (r * batch + e) * k_out
+            pre[at : at + k_out, :] = jnp.dot(
+                inv_out, right[e * k_out : (e + 1) * k_out],
+                precision=HIGHEST, preferred_element_type=F32,
+            )
     for o in range(k_out):
         flat[:, o * k_in : (o + 1) * k_in] = pre[pl.ds(o, inner, stride=k_out), :]
     precond = flat[...].astype(BF16)
@@ -243,16 +275,16 @@
         c.wait_recv()
     per = tests.shape[1]
     width = out_ref.shape[1]
-    placed = jnp.zeros((inner, width), F32)
-    for j in range(outer):
-        block = lax.dot_general(precond, tests[j], NT, preferred_element_type=F32)
-        first = (j * inner + p) * per
-        put = lax.broadcasted_iota(jnp.int32, (per, width), 1) == (
-            first + lax.broadcasted_iota(jnp.int32, (per, width), 0)
-        )
-        placed = placed + jnp.dot(
-            block, jnp.where(put, 1.0, 0.0), precision=HIGHEST, preferred_element_type=F32
-        )
+    block = lax.dot_general(
+        precond, jnp.concatenate([tests[j] for j in range(outer)], axis=0), NT,
+        preferred_element_type=F32,
+    )
+    held = lax.broadcasted_iota(jnp.int32, (outer * per, width), 0)
+    place = (lax.div(held, per) * inner + p) * per + lax.rem(held, per)
+    put = lax.broadcasted_iota(jnp.int32, (outer * per, width), 1) == place
+    placed = jnp.dot(
+        block, jnp.where(put, 1.0, 0.0), precision=HIGHEST, preferred_element_type=F32
+    )
     for e in range(inner):
         sbuf[e] = placed[e : e + 1]
     s_copies = [
@@ -269,7 +301,7 @@
     score = rbuf[0]
     for j in range(1, inner):
         score = score + rbuf[j]
-    out_ref[...] = score * scale
+    out_ref[...] = score
     for group in (test_copies, rs_copies, z_copies, g_copies, ag_copies, s_copies):
         for c in group:
             c.wait_send()
@@ -287,28 +319,29 @@
     height = k_in + k_out
     any_space = pl.BlockSpec(memory_space=pl.ANY)
     dma = pltpu.SemaphoreType.DMA
-    return pl.pallas_call(
-        functools.partial(kernel, inner, outer, chunks, float(total_tokens), scale),
+    out = pl.pallas_call(
+        functools.partial(kernel, inner, outer, chunks, float(total_tokens)),
         out_shape=jax.ShapeDtypeStruct((1, per * devices), F32),
         in_specs=[any_space] * 5,
         out_specs=pl.BlockSpec(memory_space=pltpu.VMEM),
         scratch_shapes=[
-            pltpu.VMEM((chunks, tok // chunks, x.shape[2]), BF16),
+            pltpu.VMEM((chunks, tok, x.shape[2] // chunks), BF16),
             pltpu.VMEM(g.shape[1:], BF16),
             pltpu.VMEM(proj_in.shape, BF16),
             pltpu.VMEM(proj_out.shape, BF16),
             pltpu.VMEM((outer,) + tests.shape, BF16),
             pltpu.VMEM((height, height), F32),
-            pltpu.VMEM((height, k_in), F32),
-            pltpu.VMEM((inner, height // inner, k_in), F32),
-            pltpu.VMEM((outer, height // inner, k_in), F32),
-            pltpu.VMEM((height, k_in), F32),
+            pltpu.VMEM((k_in, k_in), F32),
+            pltpu.VMEM((inner, k_in // inner, k_in), F32),
+            pltpu.VMEM((outer, k_in // inner, k_in), F32),
+            pltpu.VMEM((k_in, k_in), F32),
             pltpu.VMEM((inner, k_out, k_in), F32),
             pltpu.VMEM((inner * k_out, k_in), F32),
             pltpu.VMEM((inner, k_out * k_in), F32),
             pltpu.VMEM((inner, 1, per * devices), F32),
             pltpu.VMEM((inner, 1, per * devices), F32),
-            dma((4 + chunks,)),
+            pltpu.VMEM((tok, k_in), F32),
+            dma((5 + chunks,)),
             dma((outer,)), dma((outer,)),
             dma((inner,)), dma((inner,)),
             dma((inner,)), dma((inner,)),
@@ -320,6 +353,7 @@
             collective_id=0, has_side_effects=True, vmem_limit_bytes=56 * 1024 * 1024
         ),
     )(x[0], g[0], proj_in, proj_out, tests)
+    return out * scale
 
 
 def solution(mesh):

time: 33 us -> 29.2 us (0.88)
  Pallas kernels: 31.7 us -> 27.8 us
  other arithmetic: 0 us -> 1.19 us
  local copies, waits for them, and re-layouts: 1.19 us -> 0 us
    pallas_call x1, Pallas kernels: 31.7 us -> 27.8 us  [on_device(): pl.pallas_call(functools.partial(kernel, inner, outer, chunks, float(tota...]
    mul x0 -> x1, other arithmetic: none -> 1.19 us  [on_device(): return out * scale]
    unnamed x1 -> x0, local copies, waits for them, and re-layouts: 1.19 us -> none
where the time goes in v2:
time: 29.2 us; the launch traced here: 29 us
  Pallas kernels  27.8 us (95%)
  other arithmetic  1.19 us (4%)
    pallas_call x1, Pallas kernels, on_device(): pl.pallas_call(functools.partial(kernel, inner, outer, chunks, float(tota...  27.8 us
    mul x1, other arithmetic, on_device(): return out * scale  1.19 us

profile of v2, /device:TPU:0, one launch (start us, length us, event | category | flops | bytes accessed | tf_op | source)
XLA Modules:
  0.0 29.0 jit_solution(11233119710321315347)
XLA Ops:
  0.0 27.8 %shard_map.55 = f32[1,128]{1,0:T(1,128)} custom-call(bf16[1024,4096]{1,0:T(8,128)(2,1)} %bitcast.2, bf16[1024,1024]{1,0:T(8,128)(2,1)} %bitcast.3, bf16[128,4096]{1,0:T(8,128)(2,1)} %pin_hbm.1, bf16[64,1024]{1,0:T(8,128)(2,1)} %pout_hbm.1, bf16[4,8192]{1,0:T(4,128)(2,1)} %test_hbm.1), custom_call_target="tpu_custom_call" | custom-call | tf_op jit(solution)/shard_map/pallas_call | solution.py:322
  27.8 1.2 %broadcast_multiply_fusion = f32[1,128]{1,0:T(1,128)} fusion(f32[1,128]{1,0:T(1,128)} %shard_map.55), kind=kLoop, calls=%fused_computation | loop fusion | flops 128 | bytes 1024 | tf_op jit(solution)/shard_map/mul | solution.py:356

commit v3 on v2

--- a/solution.py
+++ b/solution.py
@@ -124,38 +124,41 @@
     for k in range(1, outer):
         pl.semaphore_signal(barrier, inc=1, device_id={"ex": at_outer(k)}, device_id_type=MESH)
 
-    loads = [
-        pltpu.make_async_copy(pout_hbm, pout_buf, in_sem.at[0]),
-        pltpu.make_async_copy(pin_hbm, pin_buf, in_sem.at[1]),
-    ]
-    own_tests = pltpu.make_async_copy(test_hbm, tests.at[z], in_sem.at[2])
+    pout_load = pltpu.make_async_copy(pout_hbm, pout_buf, in_sem.at[0])
+    own_tests = pltpu.make_async_copy(test_hbm, tests.at[z], in_sem.at[1])
+
+    def pin_load(i):
+        cols = slice(i * step_cols, (i + 1) * step_cols)
+        return pltpu.make_async_copy(
+            pin_hbm.at[:, cols], pin_buf.at[:, cols], in_sem.at[4 + chunks + i]
+        )
 
     def x_load(i):
         return pltpu.make_async_copy(
-            x_hbm.at[:, i * step_cols : (i + 1) * step_cols], x_buf.at[i], in_sem.at[5 + i]
+            x_hbm.at[:, i * step_cols : (i + 1) * step_cols], x_buf.at[i], in_sem.at[4 + i]
         )
 
     mid = g_buf.shape[0] // 2
     quarter = mid // 2
     g_loads = [
         pltpu.make_async_copy(
-            g_hbm.at[pl.ds(h * mid, mid)], g_buf.at[pl.ds(h * mid, mid)], in_sem.at[3 + h]
+            g_hbm.at[pl.ds(h * mid, mid)], g_buf.at[pl.ds(h * mid, mid)], in_sem.at[2 + h]
         )
         for h in range(2)
     ]
-    loads[0].start()
+    pout_load.start()
     for c in g_loads:
         c.start()
-    loads[1].start()
+    for i in range(chunks):
+        pin_load(i).start()
+        x_load(i).start()
     own_tests.start()
-    for i in range(chunks):
-        x_load(i).start()
 
     test_copies = [
         remote(test_hbm, tests.at[z], t_send.at[k], t_recv.at[k], at_outer(k))
         for k in range(1, outer)
     ]
-    loads[0].wait()
+    pout_load.wait()
     halves = (slice(0, mid), slice(mid, 2 * mid))
     backs = []
     for h in range(2):
@@ -166,13 +169,12 @@
             ).astype(BF16)
             for q in (h * mid, h * mid + quarter)
         ]
-    loads[1].wait()
+    pl.semaphore_wait(barrier, inner + outer - 2)
+    for c in test_copies:
+        c.start()
     for i in range(chunks):
+        pin_load(i).wait()
         x_load(i).wait()
-        if i == 1:
-            pl.semaphore_wait(barrier, inner + outer - 2)
-            for c in test_copies:
-                c.start()
         weights = pin_buf[:, i * step_cols : (i + 1) * step_cols]
         feats = [
             lax.dot_general(x_buf[i, h, :], weights, NT, preferred_element_type=F32)
@@ -224,6 +226,8 @@
         remote(grads.at[p], grads.at[p], g_send.at[k], g_recv.at[k], at_inner(k))
         for k in range(1, inner)
     ]
+    for c in g_copies:
+        c.start()
     for c in z_copies:
         c.wait_recv()
     total = z_buf[0]
@@ -235,8 +239,6 @@
         remote(mine, mine, ag_send.at[k], ag_recv.at[k], at_inner(k)) for k in range(1, inner)
     ]
     for c in ag_copies:
-        c.start()
-    for c in g_copies:
         c.start()
     for c in ag_copies:
         c.wait_recv()
@@ -313,7 +315,7 @@
     inner = math.gcd(devices, 8)
     outer = devices // inner
     per = tests.shape[0]
-    chunks = 4
+    chunks = 8
     total_tokens = tok * devices
     scale = 4.0 / (k_in * k_out * tok) ** 0.5
     height = k_in + k_out
@@ -341,7 +343,7 @@
             pltpu.VMEM((inner, 1, per * devices), F32),
             pltpu.VMEM((inner, 1, per * devices), F32),
             pltpu.VMEM((tok, k_in), F32),
-            dma((5 + chunks,)),
+            dma((4 + 2 * chunks,)),
             dma((outer,)), dma((outer,)),
             dma((inner,)), dma((inner,)),
             dma((inner,)), dma((inner,)),

time: 29.2 us -> 28.7 us (0.983)
  Pallas kernels: 27.8 us -> 27.4 us
    pallas_call x1, Pallas kernels: 27.8 us -> 27.4 us  [on_device(): pl.pallas_call(functools.partial(kernel, inner, outer, chunks, float(tota...]
where the time goes in v3:
time: 28.7 us; the launch traced here: 28.6 us
  Pallas kernels  27.4 us (95%)
  other arithmetic  1.19 us (4%)
    pallas_call x1, Pallas kernels, on_device(): pl.pallas_call(functools.partial(kernel, inner, outer, chunks, float(tota...  27.4 us
    mul x1, other arithmetic, on_device(): return out * scale  1.19 us

profile of v3, /device:TPU:0, one launch (start us, length us, event | category | flops | bytes accessed | tf_op | source)
XLA Modules:
  0.0 28.6 jit_solution(2900596854364315158)
XLA Ops:
  0.0 27.4 %shard_map.55 = f32[1,128]{1,0:T(1,128)} custom-call(bf16[1024,4096]{1,0:T(8,128)(2,1)} %bitcast.2, bf16[1024,1024]{1,0:T(8,128)(2,1)} %bitcast.3, bf16[128,4096]{1,0:T(8,128)(2,1)} %pin_hbm.1, bf16[64,1024]{1,0:T(8,128)(2,1)} %pout_hbm.1, bf16[4,8192]{1,0:T(4,128)(2,1)} %test_hbm.1), custom_call_target="tpu_custom_call" | custom-call | tf_op jit(solution)/shard_map/pallas_call | solution.py:324
  27.4 1.2 %broadcast_multiply_fusion = f32[1,128]{1,0:T(1,128)} fusion(f32[1,128]{1,0:T(1,128)} %shard_map.55), kind=kLoop, calls=%fused_computation | loop fusion | flops 128 | bytes 1024 | tf_op jit(solution)/shard_map/mul | solution.py:358

commit v4 on v3

--- a/solution.py
+++ b/solution.py
@@ -183,12 +183,13 @@
         for h, feat in zip(halves, feats):
             if i == 0:
                 acc[h, :] = feat
-            else:
+            elif i < chunks - 1:
                 acc[h, :] += feat
+    lasts = [acc[h, :] + feat for h, feat in zip(halves, feats)]
     parts = []
     for h in range(2):
         back = jnp.concatenate(backs[2 * h : 2 * h + 2], axis=0)
-        both = jnp.concatenate([acc[halves[h], :].astype(BF16), back], axis=1)
+        both = jnp.concatenate([lasts[h].astype(BF16), back], axis=1)
         parts.append(lax.dot_general(both, both, TN, preferred_element_type=F32))
     cov[...] = parts[0] + parts[1]
 

time: 28.7 us -> 28.7 us (level)
  no operation moved by 1% of the time
where the time goes in v4:
time: 28.7 us; the launch traced here: 28.6 us
  Pallas kernels  27.4 us (95%)
  other arithmetic  1.19 us (4%)
    pallas_call x1, Pallas kernels, on_device(): pl.pallas_call(functools.partial(kernel, inner, outer, chunks, float(tota...  27.4 us
    mul x1, other arithmetic, on_device(): return out * scale  1.19 us

profile of v4, /device:TPU:0, one launch (start us, length us, event | category | flops | bytes accessed | tf_op | source)
XLA Modules:
  0.0 28.6 jit_solution(2900596854364315158)
XLA Ops:
  0.0 27.4 %shard_map.55 = f32[1,128]{1,0:T(1,128)} custom-call(bf16[1024,4096]{1,0:T(8,128)(2,1)} %bitcast.2, bf16[1024,1024]{1,0:T(8,128)(2,1)} %bitcast.3, bf16[128,4096]{1,0:T(8,128)(2,1)} %pin_hbm.1, bf16[64,1024]{1,0:T(8,128)(2,1)} %pout_hbm.1, bf16[4,8192]{1,0:T(4,128)(2,1)} %test_hbm.1), custom_call_target="tpu_custom_call" | custom-call | tf_op jit(solution)/shard_map/pallas_call | solution.py:325
  27.4 1.2 %broadcast_multiply_fusion = f32[1,128]{1,0:T(1,128)} fusion(f32[1,128]{1,0:T(1,128)} %shard_map.55), kind=kLoop, calls=%fused_computation | loop fusion | flops 128 | bytes 1024 | tf_op jit(solution)/shard_map/mul | solution.py:359
